TPU v7x, 512 devices: a whole 4x4x16 slice. The times are simulated.
512 devices in a mesh: row: 16 (over x, y), col: 32 (over z, core).
Axes of the slice: x: 4, y: 4, z: 16, core: 2. Of those that a mesh axis runs over, the one named last changes fastest.
Arguments:
- object_field: float32 [2, 2048, 4096], P(None, 'row', 'col'), may hold values from -5 to 5
- probe_modes: float32 [2, 2, 128, 128], replicated, may hold values from -5 to 5
- amplitudes: float32 [16, 32, 2, 128, 128], P('row', 'col'), may hold values from 0.5 to 4
- positions: int32 [16, 32, 2, 2], P('row', 'col'), may hold values from 0 to 127
- counts: int32 [16, 32], P('row', 'col'), may hold values from 1 to 2, as said below
Outputs:
- object_out: float32 [2, 2048, 4096], P(None, 'row', 'col')
- probe_out: float32 [2, 2, 128, 128], replicated
Inputs may be any that keep to these rules, and one draw needn't show every extreme that they name: `counts`: slots at or beyond a tile's count hold no frame; in every draw some tile has all 2 slots live.
All inputs are finite; a program needn't handle non-finite values.
Results may differ from a plain program's by a relative error of at most 0.0001.
Values sent between devices are 32-bit elements; how exact they have to be, the bound alone decides.
A program may use at most 64 MiB of HBM per device.

v0:
```python
import jax
import jax.numpy as jnp
from jax import lax
from jax.sharding import PartitionSpec as P

damping = 1.0
highest = lax.Precision.HIGHEST


def with_halo(value, sides, width):
    for axis, dim in sides:
        size, length = (lax.axis_size(axis), value.shape[dim])
        up = [(i, (i + 1) % size) for i in range(size - 1)]
        down = [(j, i) for i, j in up]
        last = lax.slice_in_dim(value, length - width, length, axis=dim)
        initial = lax.slice_in_dim(value, 0, width, axis=dim)
        before = lax.ppermute(last, axis, up)
        after = lax.ppermute(initial, axis, down)
        value = jnp.concatenate([before, value, after], axis=dim)
    return value


def dft_tables(frame_len):
    index_row = jnp.arange(frame_len, dtype=jnp.int32)
    product = index_row[:, None] * index_row[None, :] % frame_len
    angles = product.astype(jnp.float32) * (2.0 * jnp.pi / frame_len)
    norming = 1.0 / jnp.sqrt(jnp.float32(frame_len))
    return (jnp.cos(angles) * norming, jnp.sin(angles) * norming)


def right_product(values_in, table):
    return jnp.einsum("skab,bc->skac", values_in, table, precision=highest)


def left_product(table, values_in):
    return jnp.einsum("ab,skbc->skac", table, values_in, precision=highest)


def transform(real_part, imag_part, cosine_table, sine_table, direction):
    row_re = right_product(real_part, cosine_table) + direction * right_product(
        imag_part, sine_table
    )
    row_im = right_product(imag_part, cosine_table) - direction * right_product(
        real_part, sine_table
    )
    out_re = left_product(cosine_table, row_re) + direction * left_product(sine_table, row_im)
    out_im = left_product(cosine_table, row_im) - direction * left_product(sine_table, row_re)
    return (out_re, out_im)


def fetch_rim(tile_field, rim_width):
    return with_halo(tile_field, (("row", 1), ("col", 2)), rim_width)


def fold_axis(values_in, along, length, rim_width, offset):
    extent = values_in.shape[along]
    middle = lax.slice_in_dim(values_in, offset, offset + length, axis=along)
    head_part = lax.slice_in_dim(values_in, 0, rim_width, axis=along)
    bottom = lax.slice_in_dim(values_in, extent - rim_width, extent, axis=along)
    widths_head = [
        (0, length - rim_width) if which_dim == along else (0, 0)
        for which_dim in range(values_in.ndim)
    ]
    widths_tail = [
        (length - rim_width, 0) if which_dim == along else (0, 0)
        for which_dim in range(values_in.ndim)
    ]
    return middle + jnp.pad(head_part, widths_head) + jnp.pad(bottom, widths_tail)


def pass_terms(padded, probe_modes, amp_rows, top_rows, left_cols, live_mask, tables):
    frame_len = probe_modes.shape[-1]
    cosine_table, sine_table = tables
    anchor = jnp.int32(0)

    def cut_one(top_row, left_col):
        return lax.dynamic_slice(padded, (anchor, top_row, left_col), (2, frame_len, frame_len))

    patches = jax.vmap(cut_one)(top_rows, left_cols)
    o_re = patches[:, 0][:, None]
    o_im = patches[:, 1][:, None]
    p_re = probe_modes[:, 0][None]
    p_im = probe_modes[:, 1][None]
    psi_re = p_re * o_re - p_im * o_im
    psi_im = p_re * o_im + p_im * o_re
    far_re, far_im = transform(psi_re, psi_im, cosine_table, sine_table, 1.0)
    intensity = jnp.sum(far_re * far_re + far_im * far_im, axis=1)
    modulus = (amp_rows / jnp.sqrt(intensity + 1.0))[:, None]
    back_re, back_im = transform(far_re * modulus, far_im * modulus, cosine_table, sine_table, -1.0)
    live_wide = live_mask[:, None, None, None]
    d_re = (back_re - psi_re) * live_wide
    d_im = (back_im - psi_im) * live_wide
    n_re = jnp.sum(p_re * d_re + p_im * d_im, axis=1)
    n_im = jnp.sum(p_re * d_im - p_im * d_re, axis=1)
    probe_power = jnp.sum(p_re * p_re + p_im * p_im, axis=1)
    deposits = jnp.stack([n_re, n_im, live_mask[:, None, None] * probe_power], axis=1)

    def deposit(slot_index, buffer):
        top_row = top_rows[slot_index]
        left_col = left_cols[slot_index]
        existing = lax.dynamic_slice(buffer, (anchor, top_row, left_col), (3, frame_len, frame_len))
        return lax.dynamic_update_slice(
            buffer, existing + deposits[slot_index], (anchor, top_row, left_col)
        )

    buffer = jnp.zeros((3,) + padded.shape[1:], jnp.float32)
    buffer = lax.fori_loop(0, top_rows.shape[0], deposit, buffer)
    q_re = jnp.sum(o_re * d_re + o_im * d_im, axis=0)
    q_im = jnp.sum(o_re * d_im - o_im * d_re, axis=0)
    probe_num = jnp.stack([q_re, q_im], axis=1)
    probe_den = jnp.sum(
        live_mask[:, None, None] * (patches[:, 0] ** 2 + patches[:, 1] ** 2), axis=0
    )
    return (buffer, probe_num, probe_den)


def update_probe(probe_modes, probe_num, probe_den):
    total_num, total_den = lax.psum((probe_num, probe_den), ("row", "col"))
    return probe_modes + total_num / (total_den + damping)


def on_device(object_field, probe_modes, amplitudes, positions, counts):
    tile_len = object_field.shape[1]
    frame_len = probe_modes.shape[-1]
    rim_len = frame_len // 2
    slot_count = amplitudes.shape[2]
    amp_rows = amplitudes[0, 0]
    top_rows = positions[0, 0, :, 0]
    left_cols = positions[0, 0, :, 1]
    live_ints = (jnp.arange(slot_count, dtype=jnp.int32) < counts[0, 0]).astype(jnp.int32)
    live_mask = live_ints.astype(jnp.float32)
    tables = dft_tables(frame_len)
    current = object_field
    probe_now = probe_modes
    padded = fetch_rim(current, rim_len)
    buffer, probe_num, probe_den = pass_terms(
        padded, probe_now, amp_rows, top_rows, left_cols, live_mask, tables
    )
    spread = with_halo(buffer, (("row", 1), ("col", 2)), rim_len)
    summed = fold_axis(spread, 1, tile_len, rim_len, frame_len)
    summed = fold_axis(summed, 2, tile_len, rim_len, frame_len)
    current = current + summed[0:2] / (summed[2:3] + damping)
    probe_now = update_probe(probe_now, probe_num, probe_den)
    return (current, probe_now)


def solution(mesh):
    return jax.shard_map(
        on_device,
        mesh=mesh,
        in_specs=(
            P(None, "row", "col"),
            P(),
            P("row", "col", None, None, None),
            P("row", "col", None, None),
            P("row", "col"),
        ),
        out_specs=(P(None, "row", "col"), P()),
        check_vma=False,
    )
```

profile of v0, /device:TPU:1, one launch (start us, length us, event | category | flops | bytes accessed | tf_op | source)
XLA Modules:
  0.0 559.1 jit_solution(17956020790190083772)
XLA Ops:
  7.2 0.9 fusion.156
  8.1 4.0 collective-permute-start
  12.2 1.3 collective-permute-start.1
  13.5 1.0 slice_reduce_fusion
  14.6 1.0 slice_bitcast_fusion.3
  15.8 1.0 copy.73
  17.8 5.1 collective-permute-start.2
  22.9 2.9 collective-permute-start.3
  26.2 4.4 collective-permute-done.3
  30.8 3.9 while.15
  31.4 1.3 bitcast_dynamic-update-slice_fusion.2
  33.4 1.3 bitcast_dynamic-update-slice_fusion.2
  34.9 0.8 fusion.14
  35.7 0.8 fusion.15
  36.5 0.8 convolution_subtract_fusion.1
  38.0 0.8 convolution_add_fusion.1
  42.4 0.7 fusion.6
  46.1 1.0 add_reduce_fusion
  47.2 17.1 %while.14 = (s32[]{:T(128)}, f32[3,256,256]{1,2,0:T(8,128)S(1)}, s32[2]{0:T(128)S(1)}, s32[2]{0:T(128)S(1)}, f32[2,3,128,128]{2,3,0,1:T(8,128)S(1)}, /*index=5*/s32[]{:T(128)}, s32[]{:T(128)}, s32[]{:T(128)}) while((s32[]{:T(128)}, f32[3,256,256]{1,2,0:T(8,128)S(1)}, s32[2]{0:T(128)S(1)}, s32[2]{0:T(128)S(1)}, ...), condition=%wide.region_5.6_spmd, body=%wide.region_4.5_spmd.sunk | while | flops 49160 | bytes 2949313 | solution.py:107
  52.9 3.0 dynamic_update_slice.8
  61.5 2.8 dynamic_update_slice.8
  64.5 3.7 collective-permute-start.4
  68.2 1.3 collective-permute-start.5
  71.2 3.1 collective-permute-done.4
  74.3 4.1 collective-permute-done.5
  78.7 4.6 collective-permute-start.6
  83.3 1.9 collective-permute-start.7
  85.2 462.4 %all-reduce.5.cloned.1.call-done = (f32[2,2,128,128]{2,3,0,1:T(8,128)}, f32[128,128]{1,0:T(8,128)}) async-done(((f32[2,2,128,128]{2,3,0,1:T(8,128)}, f32[128,128]{1,0:T(8,128)}), (f32[2,2,128,128]{2,3,0,1:T(8,128)}, f32[128,128]{1,0:T(8,128)})) %all-reduce.5.cloned.1.call-update) | async-done | bytes 327696 | tf_op jit(solution)/shard_map/psum | solution.py:118
  547.6 0.8 broadcast_add_fusion
  548.5 1.0 divide_add_fusion
  549.5 0.8 copy.93
  551.5 0.8 copy.92
  (79 shorter events, 16.7 us)
Async XLA Ops:
  7.2 10.4 %copy-start = (f32[2,128,128]{2,1,0:T(8,128)S(1)}, f32[2,128,128]{2,1,0:T(8,128)}, u32[]{:S(2)}) copy-start(f32[2,128,128]{2,1,0:T(8,128)} %param.7) | copy-start | bytes 393220
  7.2 540.4 %all-reduce.5.cloned.1.call-start = ((), (), s32[]{:S(2)}) async-start(), calls=%async_computation | async-start | bytes 655360 | tf_op jit(solution)/shard_map/psum | solution.py:118
  8.1 9.4 %collective-permute-start = (f32[2,64,128]{2,1,0:T(8,128)S(1)}, f32[2,64,128]{2,1,0:T(8,128)S(1)}, u32[]{:S(2)}, u32[]{:S(2)}) collective-permute-start(f32[2,64,128]{2,1,0:T(8,128)S(1)} %get-tuple-element.171), channel_id=1, source_target_pairs={{0,32},{32,64},{64,96},{96,128},{128,160},{160,192},{192,224},{224... | collective-permute-start | bytes 196616 | tf_op jit(solution)/shard_map/ppermute | solution.py:17
  12.2 5.4 collective-permute-start.1
  17.8 8.4 %collective-permute-start.2 = (f32[2,256,64]{2,1,0:T(8,128)S(1)}, f32[2,256,64]{2,1,0:T(8,128)S(1)}, u32[]{:S(2)}, u32[]{:S(2)}) collective-permute-start(f32[2,256,64]{2,1,0:T(8,128)S(1)} %get-tuple-element.168), channel_id=1, source_target_pairs={{0,1},{1,2},{2,3},{3,4},{4,5},{5,6},{6,7},{7,8},{8,9},{9,10},{10,1... | collective-permute-start | bytes 393224 | tf_op jit(solution)/shard_map/ppermute | solution.py:17
  22.9 7.7 %collective-permute-start.3 = (f32[2,256,64]{2,1,0:T(8,128)S(1)}, f32[2,256,64]{2,1,0:T(8,128)S(1)}, u32[]{:S(2)}, u32[]{:S(2)}) collective-permute-start(f32[2,256,64]{2,1,0:T(8,128)S(1)} %get-tuple-element.169), channel_id=1, source_target_pairs={{1,0},{2,1},{3,2},{4,3},{5,4},{6,5},{7,6},{8,7},{9,8},{10,9},{11,1... | collective-permute-start | bytes 393224 | tf_op jit(solution)/shard_map/ppermute | solution.py:18
  64.3 6.7 %copy-start.1 = (f32[2,2,128,128]{3,2,1,0:T(8,128)S(1)}, f32[2,2,128,128]{3,2,1,0:T(8,128)}, u32[]{:S(2)}) copy-start(f32[2,2,128,128]{3,2,1,0:T(8,128)} %param.8) | copy-start | bytes 786436
  64.5 9.8 %collective-permute-start.4 = (f32[3,64,256]{1,2,0:T(8,128)S(1)}, f32[3,64,256]{1,2,0:T(8,128)S(1)}, u32[]{:S(2)}, u32[]{:S(2)}) collective-permute-start(f32[3,64,256]{1,2,0:T(8,128)S(1)} %get-tuple-element.163), channel_id=1, source_target_pairs={{0,32},{32,64},{64,96},{96,128},{128,160},{160,192},{192,224},{224... | collective-permute-start | bytes 589832 | tf_op jit(solution)/shard_map/ppermute | solution.py:17
  68.2 10.2 %collective-permute-start.5 = (f32[3,64,256]{1,2,0:T(8,128)S(1)}, f32[3,64,256]{1,2,0:T(8,128)S(1)}, u32[]{:S(2)}, u32[]{:S(2)}) collective-permute-start(f32[3,64,256]{1,2,0:T(8,128)S(1)} %get-tuple-element.164), channel_id=1, source_target_pairs={{32,0},{64,32},{96,64},{128,96},{160,128},{192,160},{224,192},{256... | collective-permute-start | bytes 589832 | tf_op jit(solution)/shard_map/ppermute | solution.py:18
  78.7 471.6 %collective-permute-start.6 = (f32[3,384,64]{1,2,0:T(8,128)S(1)}, f32[3,384,64]{1,2,0:T(8,128)S(1)}, u32[]{:S(2)}, u32[]{:S(2)}) collective-permute-start(f32[3,384,64]{1,2,0:T(8,128)S(1)} %get-tuple-element.161), channel_id=1, source_target_pairs={{0,1},{1,2},{2,3},{3,4},{4,5},{5,6},{6,7},{7,8},{8,9},{9,10},{10,1... | collective-permute-start | bytes 884744 | tf_op jit(solution)/shard_map/ppermute | solution.py:17
  83.3 467.1 %collective-permute-start.7 = (f32[3,384,64]{1,2,0:T(8,128)S(1)}, f32[3,384,64]{1,2,0:T(8,128)S(1)}, u32[]{:S(2)}, u32[]{:S(2)}) collective-permute-start(f32[3,384,64]{1,2,0:T(8,128)S(1)} %get-tuple-element.162), channel_id=1, source_target_pairs={{1,0},{2,1},{3,2},{4,3},{5,4},{6,5},{7,6},{8,7},{9,8},{10,9},{11,1... | collective-permute-start | bytes 884744 | tf_op jit(solution)/shard_map/ppermute | solution.py:18
  550.4 0.7 copy-start.2
Sparse Core Ops, SparseCore 0:
  71.1 476.4 all-reduce.4
where the time goes:
time: 560 us; the launch traced here: 559 us
  waiting for transfers between devices  474 us (85%)
  starting transfers between devices  24.9 us (4%)
  local copies, waits for them, and re-layouts  19 us (3%)
  between operations  15.2 us (3%)
  matrix products  12 us (2%)
  loops' own time  7.93 us (1%)
  other arithmetic  5.83 us (1%)
    psum x1, waiting for transfers between devices, update_probe(): total_num, total_den = lax.psum((probe_num, probe_den), ('row', 'col'))  462 us
    ppermute x4, starting transfers between devices, with_halo(): before = lax.ppermute(last, axis, up)  17.4 us
  transfers between devices with their start and end apart: 9, of which 5 were waited for; matrix products, arithmetic and copies ran while one was open for 1% of the time, Pallas kernels for 0%

commit v1 on v0

v1 whole, which is shorter than its diff:
```python
import functools

import jax
import jax.numpy as jnp
import numpy as np
from jax import lax
from jax.experimental import pallas as pl
from jax.experimental.pallas import tpu as pltpu
from jax.sharding import PartitionSpec as P

damping = 1.0
MESH = pl.DeviceIdType.MESH
f32 = jnp.float32
bf16 = jnp.bfloat16
VMEM = pl.BlockSpec(memory_space=pltpu.VMEM)
SMEM = pl.BlockSpec(memory_space=pltpu.SMEM)


def dft_parts(size):
    index = np.arange(size)
    angles = (index[:, None] * index[None, :] % size) * (2.0 * np.pi / size)
    cosine, sine = np.cos(angles) / np.sqrt(size), np.sin(angles) / np.sqrt(size)
    right = np.block([[cosine, -sine], [sine, cosine]])
    parts = []
    for table in (right, right.T):
        head = table.astype(bf16)
        parts += [head, (table - head.astype(np.float64)).astype(bf16)]
    return [jnp.asarray(part) for part in parts]


def split(value):
    head = value.astype(bf16)
    return head, (value - head.astype(f32)).astype(bf16)


def dot3(left, right):
    (lh, ll), (rh, rl) = left, right
    dot = functools.partial(jnp.dot, preferred_element_type=f32)
    return dot(lh, rh) + (dot(lh, rl) + dot(ll, rh))


def lanes(shape):
    return lax.broadcasted_iota(jnp.int32, shape, len(shape) - 1)


def halo_kernel(rows, cols, obj, mid, lft, rgt, pack_l, pack_r, send, recv):
    row, col = lax.axis_index("row"), lax.axis_index("col")
    up, dn = lax.rem(row + rows - 1, rows), lax.rem(row + 1, rows)
    le, ri = lax.rem(col + cols - 1, cols), lax.rem(col + 1, cols)
    barrier = pltpu.get_barrier_semaphore()
    around = [(up, col), (dn, col), (row, le), (row, ri), (up, le), (up, ri), (dn, le), (dn, ri)]
    for peer in around:
        pl.semaphore_signal(barrier, inc=1, device_id=peer, device_id_type=MESH)
    size = obj.shape[1]
    half = size // 2
    low = lanes((size, size)) < half
    re, im = obj[0], obj[1]
    pack_l[...] = jnp.where(low, re, pltpu.roll(im, half, 1))
    pack_r[...] = jnp.where(low, pltpu.roll(re, half, 1), im)
    pl.semaphore_wait(barrier, 8)
    first, last = pl.ds(0, half), pl.ds(half, half)
    head, body, tail = pl.ds(0, half), pl.ds(half, size), pl.ds(half + size, half)
    plan = [
        (obj.at[:, last], mid.at[:, head], (dn, col)),
        (obj.at[:, first], mid.at[:, tail], (up, col)),
        (pack_r.at[last], lft.at[head], (dn, ri)),
        (pack_l.at[last], rgt.at[head], (dn, le)),
        (pack_r.at[first], lft.at[tail], (up, ri)),
        (pack_l.at[first], rgt.at[tail], (up, le)),
        (pack_r, lft.at[body], (row, ri)),
        (pack_l, rgt.at[body], (row, le)),
    ]
    copies = []
    for i, (src, dst, peer) in enumerate(plan):
        copy = pltpu.make_async_remote_copy(
            src_ref=src,
            dst_ref=dst,
            send_sem=send.at[i],
            recv_sem=recv.at[i],
            device_id=peer,
            device_id_type=MESH,
        )
        copy.start()
        copies.append(copy)
    mid[:, body] = obj[...]
    for copy in copies:
        copy.wait()


def fetch_halo(obj, rows, cols):
    size = obj.shape[1]
    return pl.pallas_call(
        functools.partial(halo_kernel, rows, cols),
        out_shape=(
            jax.ShapeDtypeStruct((2, 2 * size, size), f32),
            jax.ShapeDtypeStruct((2 * size, size), f32),
            jax.ShapeDtypeStruct((2 * size, size), f32),
        ),
        in_specs=[VMEM],
        out_specs=(VMEM, VMEM, VMEM),
        scratch_shapes=[
            pltpu.VMEM((size, size), f32),
            pltpu.VMEM((size, size), f32),
            pltpu.SemaphoreType.DMA((8,)),
            pltpu.SemaphoreType.DMA((8,)),
        ],
        compiler_params=pltpu.CompilerParams(collective_id=0, has_side_effects=True),
        name="halo",
    )(obj)


def pass_kernel(
    rows,
    cols,
    pos,
    cnt,
    mid,
    lft,
    rgt,
    probe,
    amp,
    mh,
    ml,
    th,
    tl,
    obj_out,
    probe_out,
    pad,
    dep_c,
    dep_s,
    side_l,
    side_r,
    got_l,
    got_r,
    fold,
    got_u,
    got_d,
    terms,
    pair_in,
    pair_sum,
    plane_in,
    plane_sum,
    depth_in,
    fresh,
    gathered,
    s1,
    r1,
    s2,
    r2,
    s3,
    r3,
    s4,
    r4,
    s5,
    r5,
    s6,
    r6,
):
    row, col = lax.axis_index("row"), lax.axis_index("col")
    up, dn = lax.rem(row + rows - 1, rows), lax.rem(row + 1, rows)
    le, ri = lax.rem(col + cols - 1, cols), lax.rem(col + 1, cols)
    deep = cols // 2
    core, z = lax.rem(col, 2), lax.div(col, 2)
    mate = col + 1 - 2 * core
    other = lax.rem(col + 2 * core - 1 + cols, cols)

    barrier = pltpu.get_barrier_semaphore()
    peers = [(row, mate), (row, other)]
    for k in range(1, rows):
        peers += [(lax.rem(row + k, rows), col), (lax.rem(row + k, rows), mate)]
    for k in range(1, deep):
        peers.append((row, 2 * lax.rem(z + k, deep) + core))
    for peer in peers:
        pl.semaphore_signal(barrier, inc=1, device_id=peer, device_id_type=MESH)

    slots, size = amp.shape[0], amp.shape[1]
    modes = probe.shape[0]
    half = size // 2
    lane = lanes((size, size))
    low = lane < half

    wide = lanes((2 * size, size))
    low2 = wide < half
    line = lax.broadcasted_iota(jnp.int32, (2 * size, size), 0)
    first_row = jnp.where(row > 0, 0, half)
    end_row = jnp.where(row < rows - 1, 2 * size, half + size)
    inside = (line >= first_row) & (line < end_row)
    in_l = inside & ((wide >= half) | (wide < jnp.where(col > 0, half, 0)))
    in_r = inside & ((wide < half) | (wide >= jnp.where(col < cols - 1, half, size)))
    lft_v, rgt_v = lft[...], rgt[...]
    for ch in range(2):
        turned = pltpu.roll(mid[ch], half, 1)
        from_l = lft_v if ch == 0 else pltpu.roll(lft_v, half, 1)
        from_r = pltpu.roll(rgt_v, half, 1) if ch == 0 else rgt_v
        pad[ch, 0] = jnp.where(in_l, jnp.where(low2, from_l, turned), 0.0)
        pad[ch, 1] = jnp.where(in_r, jnp.where(low2, turned, from_r), 0.0)

    right = (mh[...], ml[...])
    left = (th[...], tl[...])
    patches, waves = [], []
    for s in range(slots):
        r, c = pos[s, 0], pos[s, 1]
        shift = lax.rem(size - c, size)
        patch = []
        for ch in range(2):
            near = pltpu.roll(pad[ch, 0, pl.ds(r, size)], shift, 1)
            far = pltpu.roll(pad[ch, 1, pl.ds(r, size)], shift, 1)
            patch.append(jnp.where(lane < size - c, near, far))
        patches.append(patch)
        for k in range(modes):
            p_re, p_im = probe[k, 0], probe[k, 1]
            waves.append(
                (p_re * patch[0] - p_im * patch[1], p_re * patch[1] + p_im * patch[0])
            )

    def columns(stacked):
        cut = [stacked[i * size : (i + 1) * size] for i in range(len(waves))]
        return jnp.concatenate(
            [jnp.concatenate([c[:, 0:size], c[:, size : 2 * size]], axis=0) for c in cut], axis=1
        )

    def rows_of(placed):
        cut = [placed[:, i * size : (i + 1) * size] for i in range(len(waves))]
        return jnp.concatenate(
            [jnp.concatenate([c[0:size], c[size : 2 * size]], axis=1) for c in cut], axis=0
        )

    stacked = jnp.concatenate([jnp.concatenate(w, axis=1) for w in waves], axis=0)
    far_field = dot3(left, split(columns(dot3(split(stacked), right))))
    shaped = []
    for s in range(slots):
        block = far_field[:, s * modes * size : (s + 1) * modes * size]
        power = block * block
        power = power[0:size] + power[size : 2 * size]
        intensity = sum(power[:, k * size : (k + 1) * size] for k in range(modes))
        modulus = amp[s] * lax.rsqrt(intensity + 1.0)
        both = jnp.concatenate([modulus, modulus], axis=0)
        shaped += [block[:, k * size : (k + 1) * size] * both for k in range(modes)]
    back = dot3(split(rows_of(dot3(right, split(jnp.concatenate(shaped, axis=1))))), left)

    zero = jnp.zeros((size, size), f32)
    probe_power = zero
    for k in range(modes):
        probe_power += probe[k, 0] * probe[k, 0] + probe[k, 1] * probe[k, 1]
    totals = [[zero, zero] for _ in range(modes)]
    density = zero
    for s in range(slots):
        live = jnp.where(s < cnt[0, 0], 1.0, 0.0)
        o_re, o_im = patches[s]
        n_re, n_im = zero, zero
        for k in range(modes):
            i = s * modes + k
            b = back[i * size : (i + 1) * size]
            d_re = (b[:, 0:size] - waves[i][0]) * live
            d_im = (b[:, size : 2 * size] - waves[i][1]) * live
            p_re, p_im = probe[k, 0], probe[k, 1]
            n_re += p_re * d_re + p_im * d_im
            n_im += p_re * d_im - p_im * d_re
            totals[k][0] += o_re * d_re + o_im * d_im
            totals[k][1] += o_re * d_im - o_im * d_re
        density += live * (o_re * o_re + o_im * o_im)
        c = pos[s, 1]
        shift = lax.rem(c + half, size)
        center = (lane < c + half) & (lane >= c - half)
        for ch, value in enumerate((n_re, n_im, live * probe_power)):
            turned = pltpu.roll(value, shift, 1)
            dep_c[s, ch, size : 2 * size] = jnp.where(center, turned, 0.0)
            dep_s[s, ch, size : 2 * size] = jnp.where(center, 0.0, turned)
            for edge in (0, 2 * size):
                dep_c[s, ch, edge : edge + size] = zero
                dep_s[s, ch, edge : edge + size] = zero

    share = size // rows
    for k in range(modes):
        for i in range(rows):
            cut = slice(i * share, (i + 1) * share)
            terms[k, i, 0] = totals[k][0][cut]
            terms[k, i, 1] = totals[k][1][cut]
            terms[k, i, 2] = density[cut]

    def placed(store, ch):
        return sum(store[s, ch, pl.ds(size - pos[s, 0], 2 * size)] for s in range(slots))

    aside = [placed(dep_s, ch) for ch in range(3)]
    turned = pltpu.roll(aside[1], half, 1)
    side_l[0 : 2 * size] = jnp.where(low2, turned, aside[0])
    side_r[0 : 2 * size] = jnp.where(low2, aside[0], turned)
    w_head, w_tail = aside[2][0:size], pltpu.roll(aside[2][size : 2 * size], half, 1)
    side_l[2 * size : 3 * size] = jnp.where(low, w_tail, w_head)
    side_r[2 * size : 3 * size] = jnp.where(low, w_head, w_tail)

    pl.semaphore_wait(barrier, len(peers))

    def send(src, dst, ssem, rsem, peer):
        copy = pltpu.make_async_remote_copy(
            src_ref=src,
            dst_ref=dst,
            send_sem=ssem,
            recv_sem=rsem,
            device_id=peer,
            device_id_type=MESH,
        )
        copy.start()
        return copy

    pending = []
    to_mate = send(terms.at[1 - core], pair_in, s1.at[0], r1.at[0], (row, mate))
    to_left = send(side_l, got_r, s5.at[0], r5.at[0], (row, le))
    to_right = send(side_r, got_l, s5.at[1], r5.at[1], (row, ri))
    to_mate.wait()
    pair_sum[...] = terms[core] + pair_in[...]

    plane = []
    for k in range(1, rows):
        peer = lax.rem(row + k, rows)
        plane.append(
            send(pair_sum.at[peer], plane_in.at[row], s2.at[k], r2.at[k], (peer, col))
        )
    plane_in[row] = pair_sum[row]
    for copy in plane:
        copy.wait()
    reduced = plane_in[0]
    for i in range(1, rows):
        reduced += plane_in[i]
    plane_sum[...] = reduced

    depth = []
    for k in range(1, deep):
        peer = 2 * lax.rem(z + k, deep) + core
        depth.append(send(plane_sum, depth_in.at[z], s3.at[k], r3.at[k], (row, peer)))
    depth_in[z] = plane_sum[...]

    to_left.wait()
    to_right.wait()
    high = jnp.where(col < cols - 1, 1.0, 0.0)
    base = jnp.where(col > 0, 1.0, 0.0)
    by_l, by_r = got_l[...] * base, got_r[...] * high
    low3 = lanes((3 * size, size)) < half
    plain = jnp.where(low3, by_l, by_r)
    crossed = pltpu.roll(jnp.where(low3, by_r, by_l), half, 1)
    fold[0] = placed(dep_c, 0) + plain[0 : 2 * size]
    fold[1] = placed(dep_c, 1) + crossed[0 : 2 * size]
    weights = jnp.concatenate([plain[2 * size : 3 * size], crossed[2 * size : 3 * size]], axis=0)
    fold[2] = placed(dep_c, 2) + weights
    to_up = send(fold.at[:, 0:half], got_d, s6.at[0], r6.at[0], (up, col))
    to_dn = send(
        fold.at[:, half + size : 2 * size], got_u, s6.at[1], r6.at[1], (dn, col)
    )

    for copy in depth:
        copy.wait()
    total = depth_in[0]
    for i in range(1, deep):
        total += depth_in[i]
    for ch in range(2):
        cut = pl.ds(pl.multiple_of(row * share, share), share)
        fresh[ch] = probe[core, ch, cut] + total[ch] / (total[2] + damping)

    spread = [send(fresh, gathered.at[core, row], s4.at[0], r4.at[0], (row, mate))]
    for k in range(1, rows):
        peer = lax.rem(row + k, rows)
        for j, target in enumerate((col, mate)):
            i = 2 * k + j
            spread.append(
                send(fresh, gathered.at[core, row], s4.at[i], r4.at[i], (peer, target))
            )
    gathered[core, row] = fresh[...]

    to_up.wait()
    to_dn.wait()
    above = got_u[...] * jnp.where(row > 0, 1.0, 0.0)
    below = got_d[...] * jnp.where(row < rows - 1, 1.0, 0.0)
    summed = fold[:, half : half + size] + jnp.concatenate([above, below], axis=1)
    obj_out[...] = mid[:, half : half + size] + summed[0:2] / (summed[2:3] + damping)

    for copy in spread:
        copy.wait()
    for k in range(modes):
        for i in range(rows):
            for ch in range(2):
                probe_out[k, ch, i * share : (i + 1) * share] = gathered[k, i, ch]


def run_pass(pos, cnt, halo, probe, amp, rows, cols):
    slots, size = amp.shape[0], amp.shape[1]
    modes = probe.shape[0]
    deep, share, half = cols // 2, size // rows, size // 2
    dma = pltpu.SemaphoreType.DMA
    return pl.pallas_call(
        functools.partial(pass_kernel, rows, cols),
        out_shape=(
            jax.ShapeDtypeStruct((2, size, size), f32),
            jax.ShapeDtypeStruct(probe.shape, f32),
        ),
        in_specs=[SMEM, SMEM] + [VMEM] * 9,
        out_specs=(VMEM, VMEM),
        scratch_shapes=[
            pltpu.VMEM((2, 2, 2 * size, size), f32),
            pltpu.VMEM((slots, 3, 3 * size, size), f32),
            pltpu.VMEM((slots, 3, 3 * size, size), f32),
            pltpu.VMEM((3 * size, size), f32),
            pltpu.VMEM((3 * size, size), f32),
            pltpu.VMEM((3 * size, size), f32),
            pltpu.VMEM((3 * size, size), f32),
            pltpu.VMEM((3, 2 * size, size), f32),
            pltpu.VMEM((3, half, size), f32),
            pltpu.VMEM((3, half, size), f32),
            pltpu.VMEM((modes, rows, 3, share, size), f32),
            pltpu.VMEM((rows, 3, share, size), f32),
            pltpu.VMEM((rows, 3, share, size), f32),
            pltpu.VMEM((rows, 3, share, size), f32),
            pltpu.VMEM((3, share, size), f32),
            pltpu.VMEM((deep, 3, share, size), f32),
            pltpu.VMEM((2, share, size), f32),
            pltpu.VMEM((modes, rows, 2, share, size), f32),
            dma((1,)),
            dma((1,)),
            dma((rows,)),
            dma((rows,)),
            dma((deep,)),
            dma((deep,)),
            dma((2 * rows,)),
            dma((2 * rows,)),
            dma((2,)),
            dma((2,)),
            dma((2,)),
            dma((2,)),
        ],
        compiler_params=pltpu.CompilerParams(collective_id=1, has_side_effects=True),
        name="object_pass",
    )(pos, cnt, *halo, probe, amp, *dft_parts(size))


def on_device(rows, cols, object_field, probe_modes, amplitudes, positions, counts):
    halo = fetch_halo(object_field, rows, cols)
    return run_pass(positions[0, 0], counts, halo, probe_modes, amplitudes[0, 0], rows, cols)


def solution(mesh):
    rows, cols = mesh.shape["row"], mesh.shape["col"]
    return jax.shard_map(
        functools.partial(on_device, rows, cols),
        mesh=mesh,
        in_specs=(
            P(None, "row", "col"),
            P(),
            P("row", "col", None, None, None),
            P("row", "col", None, None),
            P("row", "col"),
        ),
        out_specs=(P(None, "row", "col"), P()),
        check_vma=False,
    )
```

time: 560 us -> 60.2 us (0.11)
  waiting for transfers between devices: 474 us -> 0 us
  Pallas kernels: 0 us -> 56.4 us
  starting transfers between devices: 24.9 us -> 0 us
  local copies, waits for them, and re-layouts: 19 us -> 2.32 us
  between operations: 15.2 us -> 1.3 us
  matrix products: 12 us -> 0 us
  loops' own time: 7.93 us -> 0 us
  other arithmetic: 5.83 us -> 0 us
    psum x1 -> x0, waiting for transfers between devices: 462 us -> none  [update_probe(): total_num, total_den = lax.psum((probe_num, probe_den), ('row', 'col'))]
    pallas_call x0 -> x2, Pallas kernels: none -> 56.4 us  [the longest x1 35.8 us: run_pass(): pl.pallas_call(functools.partial(pass_kernel, rows, cols), out_shape=(jax...]
    ppermute x8 -> x0, starting transfers between devices: 24.8 us -> none  [the longest x4 17.4 us: with_halo(): before = lax.ppermute(last, axis, up)]
    dot_general x16 -> x0, matrix products: 12 us -> none  [the longest x8 6.04 us: left_product(): return jnp.einsum('ab,skbc->skac', table, values_in, precision=highest)]
    ppermute x8 -> x0, waiting for transfers between devices: 11.9 us -> none  [the longest x4 8.52 us: with_halo(): after = lax.ppermute(initial, axis, down)]
    another operation x2 -> x0, loops' own time: 7.93 us -> none  [the longest x1 7.88 us: pass_terms(): buffer = lax.fori_loop(0, top_rows.shape[0], deposit, buffer)]
    dynamic_update_slice x4 -> x0, local copies, waits for them, and re-layouts: 6.01 us -> none  [deposit(): lax.dynamic_update_slice(buffer, existing + deposits[slot_index], (anchor...]
  transfers between devices with their start and end apart: 9 -> 0, of which waited for: 5 -> 0; matrix products, arithmetic and copies ran while one was open for 1% -> 0% of each run, Pallas kernels for 0% -> 0%
where the time goes in v1:
time: 60.2 us; the launch traced here: 60 us
  Pallas kernels  56.4 us (94%)
  local copies, waits for them, and re-layouts  2.32 us (4%)
  between operations  1.3 us (2%)
    pallas_call x1, Pallas kernels, run_pass(): pl.pallas_call(functools.partial(pass_kernel, rows, cols), out_shape=(jax...  35.8 us
    pallas_call x1, Pallas kernels, fetch_halo(): pl.pallas_call(functools.partial(halo_kernel, rows, cols), out_shape=(jax...  20.6 us
    unnamed x4, local copies, waits for them, and re-layouts  2.32 us

profile of v1, /device:TPU:1, one launch (start us, length us, event | category | flops | bytes accessed | tf_op | source)
XLA Modules:
  0.0 60.0 jit_solution(5660328233577647257)
XLA Ops:
  1.3 20.6 %halo.1 = (f32[2,256,128]{2,1,0:T(8,128)}, f32[256,128]{1,0:T(8,128)}, f32[256,128]{1,0:T(8,128)}) custom-call(f32[2,128,128]{2,1,0:T(8,128)} %obj.1), custom_call_target="tpu_custom_call" | custom-call | tf_op jit(solution)/shard_map/halo/pallas_call | solution.py:92
  21.9 35.8 %object_pass.1 = (f32[2,128,128]{2,1,0:T(8,128)}, f32[2,2,128,128]{3,2,1,0:T(8,128)}) custom-call(s32[2,2]{1,0:T(2,128)} %bitcast.3, s32[1,1]{1,0:T(1,128)S(6)} %copy.13.cnt, f32[2,256,128]{2,1,0:T(8,128)} %get-tuple-element.5.mid, f32[256,128]{1,0:T(8,128)} %get-tuple-element.6.lft, f32[256,128]{1,0:T(8,128)} %get-tuple-element.7.rgt, ...), custom_call_target="tpu_custom_call" | custom-call | tf_op jit(solution)/shard_map/object_pass/pallas_call | solution.py:389
  57.7 0.0 copy-start
  57.7 1.6 %copy.14 = f32[2,128,128]{2,1,0:T(8,128)} copy(f32[2,128,128]{2,1,0:T(8,128)} %get-tuple-element.10) | data formatting | bytes 262144
  59.3 0.0 copy-done
  59.3 0.7 %copy.15 = f32[2,2,128,128]{3,2,1,0:T(8,128)} copy(f32[2,2,128,128]{3,2,1,0:T(8,128)S(1)} %copy-done) | data formatting | bytes 524288
Async XLA Ops:
  57.7 1.6 %copy-start = (f32[2,2,128,128]{3,2,1,0:T(8,128)S(1)}, f32[2,2,128,128]{3,2,1,0:T(8,128)}, u32[]{:S(2)}) copy-start(f32[2,2,128,128]{3,2,1,0:T(8,128)} %get-tuple-element.11) | copy-start | bytes 786436

commit v2 on v1

--- a/solution.py
+++ b/solution.py
@@ -1,4 +1,5 @@
 import functools
+import math
 
 import jax
 import jax.numpy as jnp
@@ -14,6 +15,7 @@
 bf16 = jnp.bfloat16
 VMEM = pl.BlockSpec(memory_space=pltpu.VMEM)
 SMEM = pl.BlockSpec(memory_space=pltpu.SMEM)
+HBM = pl.BlockSpec(memory_space=pltpu.HBM)
 
 
 def dft_parts(size):
@@ -25,7 +27,7 @@
     for table in (right, right.T):
         head = table.astype(bf16)
         parts += [head, (table - head.astype(np.float64)).astype(bf16)]
-    return [jnp.asarray(part) for part in parts]
+    return jnp.asarray(np.stack(parts))
 
 
 def split(value):
@@ -41,72 +43,6 @@
 
 def lanes(shape):
     return lax.broadcasted_iota(jnp.int32, shape, len(shape) - 1)
-
-
-def halo_kernel(rows, cols, obj, mid, lft, rgt, pack_l, pack_r, send, recv):
-    row, col = lax.axis_index("row"), lax.axis_index("col")
-    up, dn = lax.rem(row + rows - 1, rows), lax.rem(row + 1, rows)
-    le, ri = lax.rem(col + cols - 1, cols), lax.rem(col + 1, cols)
-    barrier = pltpu.get_barrier_semaphore()
-    around = [(up, col), (dn, col), (row, le), (row, ri), (up, le), (up, ri), (dn, le), (dn, ri)]
-    for peer in around:
-        pl.semaphore_signal(barrier, inc=1, device_id=peer, device_id_type=MESH)
-    size = obj.shape[1]
-    half = size // 2
-    low = lanes((size, size)) < half
-    re, im = obj[0], obj[1]
-    pack_l[...] = jnp.where(low, re, pltpu.roll(im, half, 1))
-    pack_r[...] = jnp.where(low, pltpu.roll(re, half, 1), im)
-    pl.semaphore_wait(barrier, 8)
-    first, last = pl.ds(0, half), pl.ds(half, half)
-    head, body, tail = pl.ds(0, half), pl.ds(half, size), pl.ds(half + size, half)
-    plan = [
-        (obj.at[:, last], mid.at[:, head], (dn, col)),
-        (obj.at[:, first], mid.at[:, tail], (up, col)),
-        (pack_r.at[last], lft.at[head], (dn, ri)),
-        (pack_l.at[last], rgt.at[head], (dn, le)),
-        (pack_r.at[first], lft.at[tail], (up, ri)),
-        (pack_l.at[first], rgt.at[tail], (up, le)),
-        (pack_r, lft.at[body], (row, ri)),
-        (pack_l, rgt.at[body], (row, le)),
-    ]
-    copies = []
-    for i, (src, dst, peer) in enumerate(plan):
-        copy = pltpu.make_async_remote_copy(
-            src_ref=src,
-            dst_ref=dst,
-            send_sem=send.at[i],
-            recv_sem=recv.at[i],
-            device_id=peer,
-            device_id_type=MESH,
-        )
-        copy.start()
-        copies.append(copy)
-    mid[:, body] = obj[...]
-    for copy in copies:
-        copy.wait()
-
-
-def fetch_halo(obj, rows, cols):
-    size = obj.shape[1]
-    return pl.pallas_call(
-        functools.partial(halo_kernel, rows, cols),
-        out_shape=(
-            jax.ShapeDtypeStruct((2, 2 * size, size), f32),
-            jax.ShapeDtypeStruct((2 * size, size), f32),
-            jax.ShapeDtypeStruct((2 * size, size), f32),
-        ),
-        in_specs=[VMEM],
-        out_specs=(VMEM, VMEM, VMEM),
-        scratch_shapes=[
-            pltpu.VMEM((size, size), f32),
-            pltpu.VMEM((size, size), f32),
-            pltpu.SemaphoreType.DMA((8,)),
-            pltpu.SemaphoreType.DMA((8,)),
-        ],
-        compiler_params=pltpu.CompilerParams(collective_id=0, has_side_effects=True),
-        name="halo",
-    )(obj)
 
 
 def pass_kernel(
@@ -114,17 +50,21 @@
     cols,
     pos,
     cnt,
+    obj_in,
+    probe_in,
+    amp_in,
+    tables_in,
+    obj_out,
+    gathered,
+    obj,
+    probe,
+    amp,
+    tables,
+    pack_l,
+    pack_r,
     mid,
     lft,
     rgt,
-    probe,
-    amp,
-    mh,
-    ml,
-    th,
-    tl,
-    obj_out,
-    probe_out,
     pad,
     dep_c,
     dep_s,
@@ -142,7 +82,9 @@
     plane_sum,
     depth_in,
     fresh,
-    gathered,
+    rel,
+    s0,
+    r0,
     s1,
     r1,
     s2,
@@ -163,21 +105,103 @@
     core, z = lax.rem(col, 2), lax.div(col, 2)
     mate = col + 1 - 2 * core
     other = lax.rem(col + 2 * core - 1 + cols, cols)
+    above_z = 2 * lax.rem(z + 1, deep) + core
+    below_z = 2 * lax.rem(z + deep - 1, deep) + core
+
+    side = math.isqrt(rows)
+    x, y = lax.div(row, side), lax.rem(row, side)
+
+    def hops(d, n):
+        return min(d, n - d)
+
+    offsets = sorted(
+        ((dx, dy) for dx in range(side) for dy in range(side) if dx or dy),
+        key=lambda o: (-hops(o[0], side) - hops(o[1], side), o),
+    )
+    plane_peers = [
+        (dx * side + dy, lax.rem(x + dx, side) * side + lax.rem(y + dy, side))
+        for dx, dy in offsets
+    ]
+    depth_peers = [
+        (k, 2 * lax.rem(z + k, deep) + core)
+        for k in sorted(range(1, deep), key=lambda k: (-hops(k, deep), k))
+    ]
 
     barrier = pltpu.get_barrier_semaphore()
-    peers = [(row, mate), (row, other)]
-    for k in range(1, rows):
-        peers += [(lax.rem(row + k, rows), col), (lax.rem(row + k, rows), mate)]
-    for k in range(1, deep):
-        peers.append((row, 2 * lax.rem(z + k, deep) + core))
-    for peer in peers:
+    near = [(row, mate), (row, other), (up, other), (dn, other), (row, above_z), (row, below_z)]
+    for _, peer in plane_peers:
+        near += [(peer, col), (peer, mate)]
+    for peer in near:
         pl.semaphore_signal(barrier, inc=1, device_id=peer, device_id_type=MESH)
+
+    def send(src, dst, ssem, rsem, peer):
+        copy = pltpu.make_async_remote_copy(
+            src_ref=src,
+            dst_ref=dst,
+            send_sem=ssem,
+            recv_sem=rsem,
+            device_id=peer,
+            device_id_type=MESH,
+        )
+        copy.start()
+        return copy
+
+    fetches = []
+    for i, (src, dst) in enumerate(
+        ((obj_in, obj), (probe_in, probe), (tables_in, tables), (amp_in, amp))
+    ):
+        fetch = pltpu.make_async_copy(src, dst, s0.at[8 + i])
+        fetch.start()
+        fetches.append(fetch)
 
     slots, size = amp.shape[0], amp.shape[1]
     modes = probe.shape[0]
     half = size // 2
     lane = lanes((size, size))
     low = lane < half
+
+    fetches[0].wait()
+    re, im = obj[0], obj[1]
+    pack_l[...] = jnp.where(low, re, pltpu.roll(im, half, 1))
+    pack_r[...] = jnp.where(low, pltpu.roll(re, half, 1), im)
+    pl.semaphore_wait(barrier, len(near))
+
+    left_over = [deep // 2 - 1]
+
+    def announce():
+        pl.semaphore_signal(rel.at[0], inc=1, device_id=(row, above_z), device_id_type=MESH)
+        pl.semaphore_signal(rel.at[1], inc=1, device_id=(row, below_z), device_id_type=MESH)
+
+    def relay(times):
+        for _ in range(min(times, left_over[0])):
+            pl.semaphore_wait(rel.at[0], 1)
+            pl.semaphore_wait(rel.at[1], 1)
+            announce()
+            left_over[0] -= 1
+
+    announce()
+    first, last = pl.ds(0, half), pl.ds(half, half)
+    head, body, tail = pl.ds(0, half), pl.ds(half, size), pl.ds(half + size, half)
+    plan = [
+        (pack_r.at[last], lft.at[head], (dn, ri)),
+        (pack_l.at[last], rgt.at[head], (dn, le)),
+        (pack_r.at[first], lft.at[tail], (up, ri)),
+        (pack_l.at[first], rgt.at[tail], (up, le)),
+        (obj.at[:, last], mid.at[:, head], (dn, col)),
+        (obj.at[:, first], mid.at[:, tail], (up, col)),
+        (pack_r, lft.at[body], (row, ri)),
+        (pack_l, rgt.at[body], (row, le)),
+    ]
+    copies = [send(src, dst, s0.at[i], r0.at[i], peer) for i, (src, dst, peer) in enumerate(plan)]
+    mid[:, body] = obj[...]
+    for copy in copies[6:]:
+        copy.wait()
+    relay(1)
+    for copy in copies[:6]:
+        copy.wait()
+    relay(1)
+    for fetch in fetches[1:]:
+        fetch.wait()
 
     wide = lanes((2 * size, size))
     low2 = wide < half
@@ -195,8 +219,8 @@
         pad[ch, 0] = jnp.where(in_l, jnp.where(low2, from_l, turned), 0.0)
         pad[ch, 1] = jnp.where(in_r, jnp.where(low2, turned, from_r), 0.0)
 
-    right = (mh[...], ml[...])
-    left = (th[...], tl[...])
+    right = (tables[0], tables[1])
+    left = (tables[2], tables[3])
     patches, waves = [], []
     for s in range(slots):
         r, c = pos[s, 0], pos[s, 1]
@@ -289,34 +313,19 @@
     side_l[2 * size : 3 * size] = jnp.where(low, w_tail, w_head)
     side_r[2 * size : 3 * size] = jnp.where(low, w_head, w_tail)
 
-    pl.semaphore_wait(barrier, len(peers))
-
-    def send(src, dst, ssem, rsem, peer):
-        copy = pltpu.make_async_remote_copy(
-            src_ref=src,
-            dst_ref=dst,
-            send_sem=ssem,
-            recv_sem=rsem,
-            device_id=peer,
-            device_id_type=MESH,
-        )
-        copy.start()
-        return copy
-
-    pending = []
     to_mate = send(terms.at[1 - core], pair_in, s1.at[0], r1.at[0], (row, mate))
     to_left = send(side_l, got_r, s5.at[0], r5.at[0], (row, le))
     to_right = send(side_r, got_l, s5.at[1], r5.at[1], (row, ri))
+    relay(2)
     to_mate.wait()
     pair_sum[...] = terms[core] + pair_in[...]
 
-    plane = []
-    for k in range(1, rows):
-        peer = lax.rem(row + k, rows)
-        plane.append(
-            send(pair_sum.at[peer], plane_in.at[row], s2.at[k], r2.at[k], (peer, col))
-        )
+    plane = [
+        send(pair_sum.at[peer], plane_in.at[row], s2.at[k], r2.at[k], (peer, col))
+        for k, peer in plane_peers
+    ]
     plane_in[row] = pair_sum[row]
+    relay(deep)
     for copy in plane:
         copy.wait()
     reduced = plane_in[0]
@@ -324,10 +333,11 @@
         reduced += plane_in[i]
     plane_sum[...] = reduced
 
-    depth = []
-    for k in range(1, deep):
-        peer = 2 * lax.rem(z + k, deep) + core
-        depth.append(send(plane_sum, depth_in.at[z], s3.at[k], r3.at[k], (row, peer)))
+    pl.semaphore_wait(rel.at[0], 1)
+    pl.semaphore_wait(rel.at[1], 1)
+    depth = [
+        send(plane_sum, depth_in.at[z], s3.at[k], r3.at[k], (row, peer)) for k, peer in depth_peers
+    ]
     depth_in[z] = plane_sum[...]
 
     to_left.wait()
@@ -357,8 +367,7 @@
         fresh[ch] = probe[core, ch, cut] + total[ch] / (total[2] + damping)
 
     spread = [send(fresh, gathered.at[core, row], s4.at[0], r4.at[0], (row, mate))]
-    for k in range(1, rows):
-        peer = lax.rem(row + k, rows)
+    for k, peer in plane_peers:
         for j, target in enumerate((col, mate)):
             i = 2 * k + j
             spread.append(
@@ -371,30 +380,45 @@
     above = got_u[...] * jnp.where(row > 0, 1.0, 0.0)
     below = got_d[...] * jnp.where(row < rows - 1, 1.0, 0.0)
     summed = fold[:, half : half + size] + jnp.concatenate([above, below], axis=1)
-    obj_out[...] = mid[:, half : half + size] + summed[0:2] / (summed[2:3] + damping)
+    obj_out[...] = obj[...] + summed[0:2] / (summed[2:3] + damping)
 
     for copy in spread:
         copy.wait()
+
+
+def finish_kernel(new_obj, gathered, obj_out, probe_out):
+    obj_out[...] = new_obj[...]
+    modes, rows, _, share, _ = gathered.shape
     for k in range(modes):
         for i in range(rows):
             for ch in range(2):
                 probe_out[k, ch, i * share : (i + 1) * share] = gathered[k, i, ch]
 
 
-def run_pass(pos, cnt, halo, probe, amp, rows, cols):
+def run_pass(pos, cnt, obj, probe, amp, rows, cols):
     slots, size = amp.shape[0], amp.shape[1]
     modes = probe.shape[0]
     deep, share, half = cols // 2, size // rows, size // 2
     dma = pltpu.SemaphoreType.DMA
-    return pl.pallas_call(
+    tables = dft_parts(size)
+    new_obj, gathered = pl.pallas_call(
         functools.partial(pass_kernel, rows, cols),
         out_shape=(
             jax.ShapeDtypeStruct((2, size, size), f32),
-            jax.ShapeDtypeStruct(probe.shape, f32),
+            jax.ShapeDtypeStruct((modes, rows, 2, share, size), f32),
         ),
-        in_specs=[SMEM, SMEM] + [VMEM] * 9,
+        in_specs=[SMEM, SMEM] + [HBM] * 4,
         out_specs=(VMEM, VMEM),
         scratch_shapes=[
+            pltpu.VMEM((2, size, size), f32),
+            pltpu.VMEM(probe.shape, f32),
+            pltpu.VMEM(amp.shape, f32),
+            pltpu.VMEM(tables.shape, bf16),
+            pltpu.VMEM((size, size), f32),
+            pltpu.VMEM((size, size), f32),
+            pltpu.VMEM((2, 2 * size, size), f32),
+            pltpu.VMEM((2 * size, size), f32),
+            pltpu.VMEM((2 * size, size), f32),
             pltpu.VMEM((2, 2, 2 * size, size), f32),
             pltpu.VMEM((slots, 3, 3 * size, size), f32),
             pltpu.VMEM((slots, 3, 3 * size, size), f32),
@@ -412,7 +436,9 @@
             pltpu.VMEM((3, share, size), f32),
             pltpu.VMEM((deep, 3, share, size), f32),
             pltpu.VMEM((2, share, size), f32),
-            pltpu.VMEM((modes, rows, 2, share, size), f32),
+            pltpu.SemaphoreType.REGULAR((2,)),
+            dma((12,)),
+            dma((8,)),
             dma((1,)),
             dma((1,)),
             dma((rows,)),
@@ -426,14 +452,28 @@
             dma((2,)),
             dma((2,)),
         ],
-        compiler_params=pltpu.CompilerParams(collective_id=1, has_side_effects=True),
+        compiler_params=pltpu.CompilerParams(
+            collective_id=0, has_side_effects=True, vmem_limit_bytes=20 * 2**20
+        ),
         name="object_pass",
-    )(pos, cnt, *halo, probe, amp, *dft_parts(size))
+    )(pos, cnt, *(pltpu.with_memory_space_constraint(a, pltpu.HBM) for a in (obj, probe, amp, tables)))
+    return pl.pallas_call(
+        finish_kernel,
+        out_shape=(
+            jax.ShapeDtypeStruct((2, size, size), f32),
+            jax.ShapeDtypeStruct(probe.shape, f32),
+        ),
+        in_specs=[VMEM, VMEM],
+        out_specs=(VMEM, VMEM),
+        compiler_params=pltpu.CompilerParams(vmem_limit_bytes=4 * 2**20),
+        name="finish",
+    )(new_obj, gathered)
 
 
 def on_device(rows, cols, object_field, probe_modes, amplitudes, positions, counts):
-    halo = fetch_halo(object_field, rows, cols)
-    return run_pass(positions[0, 0], counts, halo, probe_modes, amplitudes[0, 0], rows, cols)
+    return run_pass(
+        positions[0, 0], counts, object_field, probe_modes, amplitudes[0, 0], rows, cols
+    )
 
 
 def solution(mesh):

time: 60.2 us -> 51.8 us (0.86)
  Pallas kernels: 56.4 us -> 49.6 us
  local copies, waits for them, and re-layouts: 2.32 us -> 0.67 us
    pallas_call x1, Pallas kernels: 20.6 us -> 0.77 us  [run_pass(): pl.pallas_call(finish_kernel, out_shape=(jax.ShapeDtypeStruct((2, size, s...]
    pallas_call x1, Pallas kernels: 35.8 us -> 48.9 us  [run_pass(): pl.pallas_call(functools.partial(pass_kernel, rows, cols), out_shape=(jax...]
    unnamed x4 -> x2, local copies, waits for them, and re-layouts: 2.32 us -> 0.67 us
where the time goes in v2:
time: 51.8 us; the launch traced here: 51.6 us
  Pallas kernels  49.6 us (96%)
  between operations  1.29 us (2%)
  local copies, waits for them, and re-layouts  0.67 us (1%)
    pallas_call x1, Pallas kernels, run_pass(): pl.pallas_call(functools.partial(pass_kernel, rows, cols), out_shape=(jax...  48.9 us

profile of v2, /device:TPU:1, one launch (start us, length us, event | category | flops | bytes accessed | tf_op | source)
XLA Modules:
  0.0 51.6 jit_solution(8610241107011798103)
XLA Ops:
  1.3 0.0 copy-start
  1.3 0.7 %copy-done = s32[1,1,2,2]{3,2,1,0:T(2,128)S(1)} copy-done((s32[1,1,2,2]{3,2,1,0:T(2,128)S(1)}, s32[1,1,2,2]{3,2,1,0:T(2,128)}, u32[]{:S(2)}) %copy-start) | copy-done | bytes 40
  2.0 48.9 %object_pass.1 = (f32[2,128,128]{2,1,0:T(8,128)S(1)}, f32[2,16,2,8,128]{4,3,2,1,0:T(8,128)S(1)}) custom-call(s32[2,2]{1,0:T(2,128)S(1)} %bitcast.2, s32[1,1]{1,0:T(1,128)S(6)} %copy.8.cnt, f32[2,128,128]{2,1,0:T(8,128)} %obj_in.1, f32[2,2,128,128]{3,2,1,0:T(8,128)} %probe_in.1, f32[2,128,128]{2,1,0:T(8,128)} %bitcast.3, ...), custom_call_target="tpu_custom_call" | custom-call | tf_op jit(solution)/shard_map/object_pass/pallas_call | solution.py:404
  50.8 0.8 %finish.1 = (f32[2,128,128]{2,1,0:T(8,128)}, f32[2,2,128,128]{3,2,1,0:T(8,128)}) custom-call(f32[2,128,128]{2,1,0:T(8,128)S(1)} %get-tuple-element.4.new_obj, f32[2,16,2,8,128]{4,3,2,1,0:T(8,128)S(1)} %get-tuple-element.5.gathered), custom_call_target="tpu_custom_call" | custom-call | tf_op jit(solution)/shard_map/finish/pallas_call | solution.py:460
Async XLA Ops:
  1.3 0.7 %copy-start = (s32[1,1,2,2]{3,2,1,0:T(2,128)S(1)}, s32[1,1,2,2]{3,2,1,0:T(2,128)}, u32[]{:S(2)}) copy-start(s32[1,1,2,2]{3,2,1,0:T(2,128)} %param.9) | copy-start | bytes 52

commit v3 on v2

--- a/solution.py
+++ b/solution.py
@@ -41,6 +41,10 @@
     return dot(lh, rh) + (dot(lh, rl) + dot(ll, rh))
 
 
+def in_hbm(value):
+    return pltpu.with_memory_space_constraint(value, pltpu.HBM)
+
+
 def lanes(shape):
     return lax.broadcasted_iota(jnp.int32, shape, len(shape) - 1)
 
@@ -48,7 +52,7 @@
 def pass_kernel(
     rows,
     cols,
-    pos,
+    pos_in,
     cnt,
     obj_in,
     probe_in,
@@ -82,6 +86,7 @@
     plane_sum,
     depth_in,
     fresh,
+    pos,
     rel,
     s0,
     r0,
@@ -104,33 +109,43 @@
     deep = cols // 2
     core, z = lax.rem(col, 2), lax.div(col, 2)
     mate = col + 1 - 2 * core
-    other = lax.rem(col + 2 * core - 1 + cols, cols)
     above_z = 2 * lax.rem(z + 1, deep) + core
     below_z = 2 * lax.rem(z + deep - 1, deep) + core
 
+    twin = col + 2 - 4 * lax.rem(z, 2)
+    half_z, odd = lax.div(z, 2), lax.rem(z, 2)
+    pairs = deep // 2
+
     side = math.isqrt(rows)
     x, y = lax.div(row, side), lax.rem(row, side)
 
     def hops(d, n):
         return min(d, n - d)
 
+    def chip(dx, dy):
+        return lax.rem(x + dx, side) * side + lax.rem(y + dy, side)
+
     offsets = sorted(
-        ((dx, dy) for dx in range(side) for dy in range(side) if dx or dy),
+        ((dx, dy) for dx in range(side) for dy in range(side)),
         key=lambda o: (-hops(o[0], side) - hops(o[1], side), o),
     )
-    plane_peers = [
-        (dx * side + dy, lax.rem(x + dx, side) * side + lax.rem(y + dy, side))
-        for dx, dy in offsets
+    plane_peers = [(dx * side + dy, chip(dx, dy)) for dx, dy in offsets]
+    depth_peers = [
+        (k, 2 * lax.rem(z + 2 * k, deep) + core)
+        for k in sorted(range(1, pairs), key=lambda k: (-hops(k, pairs), k))
     ]
-    depth_peers = [
-        (k, 2 * lax.rem(z + k, deep) + core)
-        for k in sorted(range(1, deep), key=lambda k: (-hops(k, deep), k))
+
+    barrier = pltpu.get_barrier_semaphore()
+    beside = [
+        (chip(1, 0), col),
+        (chip(side - 1, 0), col),
+        (chip(0, 1), col),
+        (chip(0, side - 1), col),
+        (row, above_z),
+        (row, below_z),
     ]
-
-    barrier = pltpu.get_barrier_semaphore()
-    near = [(row, mate), (row, other), (up, other), (dn, other), (row, above_z), (row, below_z)]
-    for _, peer in plane_peers:
-        near += [(peer, col), (peer, mate)]
+    near = [(up, col), (dn, col), (row, le), (row, ri), (up, le), (up, ri), (dn, le), (dn, ri)]
+    near += beside
     for peer in near:
         pl.semaphore_signal(barrier, inc=1, device_id=peer, device_id_type=MESH)
 
@@ -148,7 +163,13 @@
 
     fetches = []
     for i, (src, dst) in enumerate(
-        ((obj_in, obj), (probe_in, probe), (tables_in, tables), (amp_in, amp))
+        (
+            (obj_in, obj),
+            (pos_in, pos),
+            (probe_in, probe),
+            (tables_in, tables),
+            (amp_in, amp),
+        )
     ):
         fetch = pltpu.make_async_copy(src, dst, s0.at[8 + i])
         fetch.start()
@@ -166,20 +187,28 @@
     pack_r[...] = jnp.where(low, pltpu.roll(re, half, 1), im)
     pl.semaphore_wait(barrier, len(near))
 
-    left_over = [deep // 2 - 1]
-
-    def announce():
-        pl.semaphore_signal(rel.at[0], inc=1, device_id=(row, above_z), device_id_type=MESH)
-        pl.semaphore_signal(rel.at[1], inc=1, device_id=(row, below_z), device_id_type=MESH)
-
-    def relay(times):
-        for _ in range(min(times, left_over[0])):
-            pl.semaphore_wait(rel.at[0], 1)
-            pl.semaphore_wait(rel.at[1], 1)
-            announce()
-            left_over[0] -= 1
-
-    announce()
+    plane_rounds, depth_rounds = 2 * (side // 2), deep // 2 - 1
+    rounds = iter(range(1, max(plane_rounds, depth_rounds) + 1))
+
+    def ways(step):
+        plane_ways = range(4) if step <= plane_rounds else ()
+        return (*plane_ways, *((4, 5) if step <= depth_rounds else ()))
+
+    def announce(step):
+        for i in ways(step):
+            pl.semaphore_signal(
+                rel.at[i], inc=1, device_id=beside[i], device_id_type=MESH
+            )
+
+    def relay(upto):
+        for step in rounds:
+            for i in ways(step):
+                pl.semaphore_wait(rel.at[i], 1)
+            announce(step + 1)
+            if step >= upto:
+                return
+
+    announce(1)
     first, last = pl.ds(0, half), pl.ds(half, half)
     head, body, tail = pl.ds(0, half), pl.ds(half, size), pl.ds(half + size, half)
     plan = [
@@ -199,7 +228,7 @@
     relay(1)
     for copy in copies[:6]:
         copy.wait()
-    relay(1)
+    relay(2)
     for fetch in fetches[1:]:
         fetch.wait()
 
@@ -295,12 +324,14 @@
                 dep_s[s, ch, edge : edge + size] = zero
 
     share = size // rows
+    part = share // 2
     for k in range(modes):
         for i in range(rows):
-            cut = slice(i * share, (i + 1) * share)
-            terms[k, i, 0] = totals[k][0][cut]
-            terms[k, i, 1] = totals[k][1][cut]
-            terms[k, i, 2] = density[cut]
+            for j in range(2):
+                cut = slice(i * share + j * part, i * share + (j + 1) * part)
+                terms[k, i, j, 0] = totals[k][0][cut]
+                terms[k, i, j, 1] = totals[k][1][cut]
+                terms[k, i, j, 2] = density[cut]
 
     def placed(store, ch):
         return sum(store[s, ch, pl.ds(size - pos[s, 0], 2 * size)] for s in range(slots))
@@ -313,32 +344,45 @@
     side_l[2 * size : 3 * size] = jnp.where(low, w_tail, w_head)
     side_r[2 * size : 3 * size] = jnp.where(low, w_head, w_tail)
 
-    to_mate = send(terms.at[1 - core], pair_in, s1.at[0], r1.at[0], (row, mate))
+    to_mate = [
+        (send(terms.at[1 - core, peer], pair_in.at[peer], s1.at[k], r1.at[k], (row, mate)), k, peer)
+        for k, peer in plane_peers
+    ]
+    relay(plane_rounds)
+
+    plane = []
+    for copy, k, peer in to_mate:
+        copy.wait()
+        pair_sum[peer] = terms[core, peer] + pair_in[peer]
+        plane.append(
+            send(
+                pair_sum.at[peer, 1 - odd],
+                plane_in.at[odd, row],
+                s2.at[rows + k],
+                r2.at[rows + k],
+                (peer, twin),
+            )
+        )
+        if k:
+            plane.append(
+                send(pair_sum.at[peer, odd], plane_in.at[odd, row], s2.at[k], r2.at[k], (peer, col))
+            )
     to_left = send(side_l, got_r, s5.at[0], r5.at[0], (row, le))
     to_right = send(side_r, got_l, s5.at[1], r5.at[1], (row, ri))
-    relay(2)
-    to_mate.wait()
-    pair_sum[...] = terms[core] + pair_in[...]
-
-    plane = [
-        send(pair_sum.at[peer], plane_in.at[row], s2.at[k], r2.at[k], (peer, col))
-        for k, peer in plane_peers
-    ]
-    plane_in[row] = pair_sum[row]
+    plane_in[odd, row] = pair_sum[row, odd]
     relay(deep)
     for copy in plane:
         copy.wait()
-    reduced = plane_in[0]
-    for i in range(1, rows):
-        reduced += plane_in[i]
+    reduced = plane_in[0, 0]
+    for i in range(1, 2 * rows):
+        reduced += plane_in[i // rows, i % rows]
     plane_sum[...] = reduced
 
-    pl.semaphore_wait(rel.at[0], 1)
-    pl.semaphore_wait(rel.at[1], 1)
     depth = [
-        send(plane_sum, depth_in.at[z], s3.at[k], r3.at[k], (row, peer)) for k, peer in depth_peers
+        send(plane_sum, depth_in.at[half_z], s3.at[k], r3.at[k], (row, peer))
+        for k, peer in depth_peers
     ]
-    depth_in[z] = plane_sum[...]
+    depth_in[half_z] = plane_sum[...]
 
     to_left.wait()
     to_right.wait()
@@ -360,20 +404,22 @@
     for copy in depth:
         copy.wait()
     total = depth_in[0]
-    for i in range(1, deep):
+    for i in range(1, pairs):
         total += depth_in[i]
     for ch in range(2):
-        cut = pl.ds(pl.multiple_of(row * share, share), share)
+        cut = pl.ds(row * share + odd * part, part)
         fresh[ch] = probe[core, ch, cut] + total[ch] / (total[2] + damping)
 
-    spread = [send(fresh, gathered.at[core, row], s4.at[0], r4.at[0], (row, mate))]
+    spread = []
     for k, peer in plane_peers:
-        for j, target in enumerate((col, mate)):
-            i = 2 * k + j
-            spread.append(
-                send(fresh, gathered.at[core, row], s4.at[i], r4.at[i], (peer, target))
-            )
-    gathered[core, row] = fresh[...]
+        across = 2 * (half_z * 2 + 1 - odd) + 1 - core
+        for j, target in enumerate((across, twin, mate, col)):
+            if k or j < 3:
+                i = 4 * k + j
+                spread.append(
+                    send(fresh, gathered.at[core, row, odd], s4.at[i], r4.at[i], (peer, target))
+                )
+    gathered[core, row, odd] = fresh[...]
 
     to_up.wait()
     to_dn.wait()
@@ -388,26 +434,26 @@
 
 def finish_kernel(new_obj, gathered, obj_out, probe_out):
     obj_out[...] = new_obj[...]
-    modes, rows, _, share, _ = gathered.shape
+    modes, rows, _, _, part, _ = gathered.shape
     for k in range(modes):
-        for i in range(rows):
+        for i in range(2 * rows):
             for ch in range(2):
-                probe_out[k, ch, i * share : (i + 1) * share] = gathered[k, i, ch]
+                probe_out[k, ch, i * part : (i + 1) * part] = gathered[k, i // 2, i % 2, ch]
 
 
 def run_pass(pos, cnt, obj, probe, amp, rows, cols):
     slots, size = amp.shape[0], amp.shape[1]
     modes = probe.shape[0]
-    deep, share, half = cols // 2, size // rows, size // 2
+    deep, part, half = cols // 2, size // rows // 2, size // 2
     dma = pltpu.SemaphoreType.DMA
     tables = dft_parts(size)
     new_obj, gathered = pl.pallas_call(
         functools.partial(pass_kernel, rows, cols),
         out_shape=(
             jax.ShapeDtypeStruct((2, size, size), f32),
-            jax.ShapeDtypeStruct((modes, rows, 2, share, size), f32),
+            jax.ShapeDtypeStruct((modes, rows, 2, 2, part, size), f32),
         ),
-        in_specs=[SMEM, SMEM] + [HBM] * 4,
+        in_specs=[HBM, SMEM] + [HBM] * 4,
         out_specs=(VMEM, VMEM),
         scratch_shapes=[
             pltpu.VMEM((2, size, size), f32),
@@ -429,24 +475,25 @@
             pltpu.VMEM((3, 2 * size, size), f32),
             pltpu.VMEM((3, half, size), f32),
             pltpu.VMEM((3, half, size), f32),
-            pltpu.VMEM((modes, rows, 3, share, size), f32),
-            pltpu.VMEM((rows, 3, share, size), f32),
-            pltpu.VMEM((rows, 3, share, size), f32),
-            pltpu.VMEM((rows, 3, share, size), f32),
-            pltpu.VMEM((3, share, size), f32),
-            pltpu.VMEM((deep, 3, share, size), f32),
-            pltpu.VMEM((2, share, size), f32),
-            pltpu.SemaphoreType.REGULAR((2,)),
-            dma((12,)),
+            pltpu.VMEM((modes, rows, 2, 3, part, size), f32),
+            pltpu.VMEM((rows, 2, 3, part, size), f32),
+            pltpu.VMEM((rows, 2, 3, part, size), f32),
+            pltpu.VMEM((2, rows, 3, part, size), f32),
+            pltpu.VMEM((3, part, size), f32),
+            pltpu.VMEM((deep // 2, 3, part, size), f32),
+            pltpu.VMEM((2, part, size), f32),
+            pltpu.SMEM(pos.shape, jnp.int32),
+            pltpu.SemaphoreType.REGULAR((6,)),
+            dma((13,)),
             dma((8,)),
-            dma((1,)),
-            dma((1,)),
             dma((rows,)),
             dma((rows,)),
-            dma((deep,)),
-            dma((deep,)),
             dma((2 * rows,)),
             dma((2 * rows,)),
+            dma((deep // 2,)),
+            dma((deep // 2,)),
+            dma((4 * rows,)),
+            dma((4 * rows,)),
             dma((2,)),
             dma((2,)),
             dma((2,)),
@@ -456,7 +503,7 @@
             collective_id=0, has_side_effects=True, vmem_limit_bytes=20 * 2**20
         ),
         name="object_pass",
-    )(pos, cnt, *(pltpu.with_memory_space_constraint(a, pltpu.HBM) for a in (obj, probe, amp, tables)))
+    )(in_hbm(pos), cnt, in_hbm(obj), in_hbm(probe), in_hbm(amp), in_hbm(tables))
     return pl.pallas_call(
         finish_kernel,
         out_shape=(

time: 51.8 us -> 49.5 us (0.956)
  Pallas kernels: 49.6 us -> 48.1 us
  local copies, waits for them, and re-layouts: 0.67 us -> 0 us
    pallas_call x1, Pallas kernels: 48.9 us -> 47.3 us  [run_pass(): pl.pallas_call(functools.partial(pass_kernel, rows, cols), out_shape=(jax...]
    unnamed x2 -> x0, local copies, waits for them, and re-layouts: 0.67 us -> none
where the time goes in v3:
time: 49.5 us; the launch traced here: 49.3 us
  Pallas kernels  48.1 us (97%)
  between operations  1.29 us (3%)
    pallas_call x1, Pallas kernels, run_pass(): pl.pallas_call(functools.partial(pass_kernel, rows, cols), out_shape=(jax...  47.3 us

profile of v3, /device:TPU:1, one launch (start us, length us, event | category | flops | bytes accessed | tf_op | source)
XLA Modules:
  0.0 49.3 jit_solution(11210793255211559360)
XLA Ops:
  1.3 47.3 %object_pass.1 = (f32[2,128,128]{2,1,0:T(8,128)S(1)}, f32[2,16,2,2,4,128]{5,4,3,2,1,0:T(4,128)S(1)}) custom-call(s32[2,2]{1,0:T(2,128)} %bitcast.3, s32[1,1]{1,0:T(1,128)S(6)} %copy.8.cnt, f32[2,128,128]{2,1,0:T(8,128)} %obj_in.1, f32[2,2,128,128]{3,2,1,0:T(8,128)} %probe_in.1, f32[2,128,128]{2,1,0:T(8,128)} %bitcast.2, ...), custom_call_target="tpu_custom_call" | custom-call | tf_op jit(solution)/shard_map/object_pass/pallas_call | solution.py:450
  48.5 0.8 %finish.1 = (f32[2,128,128]{2,1,0:T(8,128)}, f32[2,2,128,128]{3,2,1,0:T(8,128)}) custom-call(f32[2,128,128]{2,1,0:T(8,128)S(1)} %get-tuple-element.4.new_obj, f32[2,16,2,2,4,128]{5,4,3,2,1,0:T(4,128)S(1)} %get-tuple-element.5.gathered), custom_call_target="tpu_custom_call" | custom-call | tf_op jit(solution)/shard_map/finish/pallas_call | solution.py:507

commit v4 on v3

--- a/solution.py
+++ b/solution.py
@@ -38,7 +38,9 @@
 def dot3(left, right):
     (lh, ll), (rh, rl) = left, right
     dot = functools.partial(jnp.dot, preferred_element_type=f32)
-    return dot(lh, rh) + (dot(lh, rl) + dot(ll, rh))
+    both = dot(jnp.concatenate([lh, ll], axis=0), rh)
+    rows = lh.shape[0]
+    return both[0:rows] + (dot(lh, rl) + both[rows : 2 * rows])
 
 
 def in_hbm(value):
@@ -109,9 +111,6 @@
     deep = cols // 2
     core, z = lax.rem(col, 2), lax.div(col, 2)
     mate = col + 1 - 2 * core
-    above_z = 2 * lax.rem(z + 1, deep) + core
-    below_z = 2 * lax.rem(z + deep - 1, deep) + core
-
     twin = col + 2 - 4 * lax.rem(z, 2)
     half_z, odd = lax.div(z, 2), lax.rem(z, 2)
     pairs = deep // 2
@@ -136,21 +135,25 @@
     ]
 
     barrier = pltpu.get_barrier_semaphore()
-    beside = [
-        (chip(1, 0), col),
-        (chip(side - 1, 0), col),
-        (chip(0, 1), col),
-        (chip(0, side - 1), col),
-        (row, above_z),
-        (row, below_z),
+    reach, stride = side // 2, -(-(deep // 2) // 3)
+
+    def level(d):
+        return 2 * lax.rem(z + deep + d, deep) + core
+
+    near = [(up, col), (dn, col), (row, le), (row, ri), (up, le), (up, ri), (dn, le), (dn, ri)]
+    near += [
+        (chip(dx, dy), col)
+        for dx, dy in offsets
+        if 0 < hops(dx, side) + hops(dy, side) <= reach
     ]
-    near = [(up, col), (dn, col), (row, le), (row, ri), (up, le), (up, ri), (dn, le), (dn, ri)]
-    near += beside
+    near += [(row, level(d * sign)) for d in range(1, stride + 1) for sign in (1, -1)]
+    ends = [(row, level(stride)), (row, level(-stride))]
+    told = ([(chip(reach, 0), col), (chip(0, reach), col)] + ends, [(row, twin)] + ends)
     for peer in near:
         pl.semaphore_signal(barrier, inc=1, device_id=peer, device_id_type=MESH)
 
-    def send(src, dst, ssem, rsem, peer):
-        copy = pltpu.make_async_remote_copy(
+    def link(src, dst, ssem, rsem, peer):
+        return pltpu.make_async_remote_copy(
             src_ref=src,
             dst_ref=dst,
             send_sem=ssem,
@@ -158,6 +161,9 @@
             device_id=peer,
             device_id_type=MESH,
         )
+
+    def send(*ends):
+        copy = link(*ends)
         copy.start()
         return copy
 
@@ -187,28 +193,15 @@
     pack_r[...] = jnp.where(low, pltpu.roll(re, half, 1), im)
     pl.semaphore_wait(barrier, len(near))
 
-    plane_rounds, depth_rounds = 2 * (side // 2), deep // 2 - 1
-    rounds = iter(range(1, max(plane_rounds, depth_rounds) + 1))
-
-    def ways(step):
-        plane_ways = range(4) if step <= plane_rounds else ()
-        return (*plane_ways, *((4, 5) if step <= depth_rounds else ()))
-
-    def announce(step):
-        for i in ways(step):
-            pl.semaphore_signal(
-                rel.at[i], inc=1, device_id=beside[i], device_id_type=MESH
-            )
-
-    def relay(upto):
-        for step in rounds:
-            for i in ways(step):
-                pl.semaphore_wait(rel.at[i], 1)
-            announce(step + 1)
-            if step >= upto:
-                return
-
-    announce(1)
+    def tell(step):
+        for i, peer in enumerate(told[step]):
+            pl.semaphore_signal(rel.at[step, i], inc=1, device_id=peer, device_id_type=MESH)
+
+    def hear(step):
+        for i in range(len(told[step])):
+            pl.semaphore_wait(rel.at[step, i], 1)
+
+    tell(0)
     first, last = pl.ds(0, half), pl.ds(half, half)
     head, body, tail = pl.ds(0, half), pl.ds(half, size), pl.ds(half + size, half)
     plan = [
@@ -223,12 +216,16 @@
     ]
     copies = [send(src, dst, s0.at[i], r0.at[i], peer) for i, (src, dst, peer) in enumerate(plan)]
     mid[:, body] = obj[...]
+    border = jnp.zeros((slots, 3, size, size), f32)
+    for store in (dep_c, dep_s):
+        store[:, :, 0:size] = border
+        store[:, :, 2 * size : 3 * size] = border
     for copy in copies[6:]:
         copy.wait()
-    relay(1)
+    hear(0)
+    tell(1)
     for copy in copies[:6]:
         copy.wait()
-    relay(2)
     for fetch in fetches[1:]:
         fetch.wait()
 
@@ -292,36 +289,21 @@
     back = dot3(split(rows_of(dot3(right, split(jnp.concatenate(shaped, axis=1))))), left)
 
     zero = jnp.zeros((size, size), f32)
-    probe_power = zero
-    for k in range(modes):
-        probe_power += probe[k, 0] * probe[k, 0] + probe[k, 1] * probe[k, 1]
     totals = [[zero, zero] for _ in range(modes)]
     density = zero
+    changes = []
     for s in range(slots):
         live = jnp.where(s < cnt[0, 0], 1.0, 0.0)
         o_re, o_im = patches[s]
-        n_re, n_im = zero, zero
         for k in range(modes):
             i = s * modes + k
             b = back[i * size : (i + 1) * size]
             d_re = (b[:, 0:size] - waves[i][0]) * live
             d_im = (b[:, size : 2 * size] - waves[i][1]) * live
-            p_re, p_im = probe[k, 0], probe[k, 1]
-            n_re += p_re * d_re + p_im * d_im
-            n_im += p_re * d_im - p_im * d_re
+            changes.append((d_re, d_im))
             totals[k][0] += o_re * d_re + o_im * d_im
             totals[k][1] += o_re * d_im - o_im * d_re
         density += live * (o_re * o_re + o_im * o_im)
-        c = pos[s, 1]
-        shift = lax.rem(c + half, size)
-        center = (lane < c + half) & (lane >= c - half)
-        for ch, value in enumerate((n_re, n_im, live * probe_power)):
-            turned = pltpu.roll(value, shift, 1)
-            dep_c[s, ch, size : 2 * size] = jnp.where(center, turned, 0.0)
-            dep_s[s, ch, size : 2 * size] = jnp.where(center, 0.0, turned)
-            for edge in (0, 2 * size):
-                dep_c[s, ch, edge : edge + size] = zero
-                dep_s[s, ch, edge : edge + size] = zero
 
     share = size // rows
     part = share // 2
@@ -333,6 +315,30 @@
                 terms[k, i, j, 1] = totals[k][1][cut]
                 terms[k, i, j, 2] = density[cut]
 
+    to_mate = [
+        (send(terms.at[1 - core, peer], pair_in.at[peer], s1.at[k], r1.at[k], (row, mate)), k, peer)
+        for k, peer in plane_peers
+    ]
+
+    probe_power = zero
+    for k in range(modes):
+        probe_power += probe[k, 0] * probe[k, 0] + probe[k, 1] * probe[k, 1]
+    for s in range(slots):
+        live = jnp.where(s < cnt[0, 0], 1.0, 0.0)
+        n_re, n_im = zero, zero
+        for k in range(modes):
+            d_re, d_im = changes[s * modes + k]
+            p_re, p_im = probe[k, 0], probe[k, 1]
+            n_re += p_re * d_re + p_im * d_im
+            n_im += p_re * d_im - p_im * d_re
+        c = pos[s, 1]
+        shift = lax.rem(c + half, size)
+        center = (lane < c + half) & (lane >= c - half)
+        for ch, value in enumerate((n_re, n_im, live * probe_power)):
+            turned = pltpu.roll(value, shift, 1)
+            dep_c[s, ch, size : 2 * size] = jnp.where(center, turned, 0.0)
+            dep_s[s, ch, size : 2 * size] = jnp.where(center, 0.0, turned)
+
     def placed(store, ch):
         return sum(store[s, ch, pl.ds(size - pos[s, 0], 2 * size)] for s in range(slots))
 
@@ -344,11 +350,7 @@
     side_l[2 * size : 3 * size] = jnp.where(low, w_tail, w_head)
     side_r[2 * size : 3 * size] = jnp.where(low, w_head, w_tail)
 
-    to_mate = [
-        (send(terms.at[1 - core, peer], pair_in.at[peer], s1.at[k], r1.at[k], (row, mate)), k, peer)
-        for k, peer in plane_peers
-    ]
-    relay(plane_rounds)
+    hear(1)
 
     plane = []
     for copy, k, peer in to_mate:
@@ -367,10 +369,10 @@
             plane.append(
                 send(pair_sum.at[peer, odd], plane_in.at[odd, row], s2.at[k], r2.at[k], (peer, col))
             )
+    plane_in[odd, row] = pair_sum[row, odd]
+
     to_left = send(side_l, got_r, s5.at[0], r5.at[0], (row, le))
     to_right = send(side_r, got_l, s5.at[1], r5.at[1], (row, ri))
-    plane_in[odd, row] = pair_sum[row, odd]
-    relay(deep)
     for copy in plane:
         copy.wait()
     reduced = plane_in[0, 0]
@@ -483,7 +485,7 @@
             pltpu.VMEM((deep // 2, 3, part, size), f32),
             pltpu.VMEM((2, part, size), f32),
             pltpu.SMEM(pos.shape, jnp.int32),
-            pltpu.SemaphoreType.REGULAR((6,)),
+            pltpu.SemaphoreType.REGULAR((2, 4)),
             dma((13,)),
             dma((8,)),
             dma((rows,)),

time: 49.5 us -> 47.7 us (0.964)
  Pallas kernels: 48.1 us -> 46.3 us
    pallas_call x1, Pallas kernels: 47.3 us -> 45.5 us  [run_pass(): pl.pallas_call(functools.partial(pass_kernel, rows, cols), out_shape=(jax...]
where the time goes in v4:
time: 47.7 us; the launch traced here: 47.6 us
  Pallas kernels  46.3 us (97%)
  between operations  1.29 us (3%)
    pallas_call x1, Pallas kernels, run_pass(): pl.pallas_call(functools.partial(pass_kernel, rows, cols), out_shape=(jax...  45.5 us

profile of v4, /device:TPU:1, one launch (start us, length us, event | category | flops | bytes accessed | tf_op | source)
XLA Modules:
  0.0 47.6 jit_solution(2484772021192228373)
XLA Ops:
  1.3 45.5 %object_pass.1 = (f32[2,128,128]{2,1,0:T(8,128)S(1)}, f32[2,16,2,2,4,128]{5,4,3,2,1,0:T(4,128)S(1)}) custom-call(s32[2,2]{1,0:T(2,128)} %bitcast.3, s32[1,1]{1,0:T(1,128)S(6)} %copy.8.cnt, f32[2,128,128]{2,1,0:T(8,128)} %obj_in.1, f32[2,2,128,128]{3,2,1,0:T(8,128)} %probe_in.1, f32[2,128,128]{2,1,0:T(8,128)} %bitcast.2, ...), custom_call_target="tpu_custom_call" | custom-call | tf_op jit(solution)/shard_map/object_pass/pallas_call | solution.py:452
  46.8 0.8 %finish.1 = (f32[2,128,128]{2,1,0:T(8,128)}, f32[2,2,128,128]{3,2,1,0:T(8,128)}) custom-call(f32[2,128,128]{2,1,0:T(8,128)S(1)} %get-tuple-element.4.new_obj, f32[2,16,2,2,4,128]{5,4,3,2,1,0:T(4,128)S(1)} %get-tuple-element.5.gathered), custom_call_target="tpu_custom_call" | custom-call | tf_op jit(solution)/shard_map/finish/pallas_call | solution.py:509

commit v5 on v4

--- a/solution.py
+++ b/solution.py
@@ -38,9 +38,7 @@
 def dot3(left, right):
     (lh, ll), (rh, rl) = left, right
     dot = functools.partial(jnp.dot, preferred_element_type=f32)
-    both = dot(jnp.concatenate([lh, ll], axis=0), rh)
-    rows = lh.shape[0]
-    return both[0:rows] + (dot(lh, rl) + both[rows : 2 * rows])
+    return dot(lh, rh) + (dot(lh, rl) + dot(ll, rh))
 
 
 def in_hbm(value):
@@ -434,13 +432,21 @@
         copy.wait()
 
 
-def finish_kernel(new_obj, gathered, obj_out, probe_out):
-    obj_out[...] = new_obj[...]
+def finish_kernel(new_obj, gathered, obj_out, probe_out, probe_new, sems):
+    keep = pltpu.make_async_copy(new_obj, obj_out, sems.at[0])
+    keep.start()
     modes, rows, _, _, part, _ = gathered.shape
+    stores = []
     for k in range(modes):
         for i in range(2 * rows):
             for ch in range(2):
-                probe_out[k, ch, i * part : (i + 1) * part] = gathered[k, i // 2, i % 2, ch]
+                probe_new[k, ch, i * part : (i + 1) * part] = gathered[k, i // 2, i % 2, ch]
+        store = pltpu.make_async_copy(probe_new.at[k], probe_out.at[k], sems.at[1 + k])
+        store.start()
+        stores.append(store)
+    keep.wait()
+    for store in stores:
+        store.wait()
 
 
 def run_pass(pos, cnt, obj, probe, amp, rows, cols):
@@ -513,7 +519,8 @@
             jax.ShapeDtypeStruct(probe.shape, f32),
         ),
         in_specs=[VMEM, VMEM],
-        out_specs=(VMEM, VMEM),
+        out_specs=(HBM, HBM),
+        scratch_shapes=[pltpu.VMEM(probe.shape, f32), pltpu.SemaphoreType.DMA((1 + modes,))],
         compiler_params=pltpu.CompilerParams(vmem_limit_bytes=4 * 2**20),
         name="finish",
     )(new_obj, gathered)

time: 47.7 us -> 47.6 us (level)
  no operation moved by 1% of the time
where the time goes in v5:
time: 47.6 us; the launch traced here: 47.5 us
  Pallas kernels  46.2 us (97%)
  between operations  1.29 us (3%)
    pallas_call x1, Pallas kernels, run_pass(): pl.pallas_call(functools.partial(pass_kernel, rows, cols), out_shape=(jax...  45.4 us

profile of v5, /device:TPU:1, one launch (start us, length us, event | category | flops | bytes accessed | tf_op | source)
XLA Modules:
  0.0 47.5 jit_solution(7680333839850968032)
XLA Ops:
  1.3 45.4 %object_pass.1 = (f32[2,128,128]{2,1,0:T(8,128)S(1)}, f32[2,16,2,2,4,128]{5,4,3,2,1,0:T(4,128)S(1)}) custom-call(s32[2,2]{1,0:T(2,128)} %bitcast.3, s32[1,1]{1,0:T(1,128)S(6)} %copy.8.cnt, f32[2,128,128]{2,1,0:T(8,128)} %obj_in.1, f32[2,2,128,128]{3,2,1,0:T(8,128)} %probe_in.1, f32[2,128,128]{2,1,0:T(8,128)} %bitcast.2, ...), custom_call_target="tpu_custom_call" | custom-call | tf_op jit(solution)/shard_map/object_pass/pallas_call | solution.py:458
  46.7 0.8 %finish.1 = (f32[2,128,128]{2,1,0:T(8,128)}, f32[2,2,128,128]{3,2,1,0:T(8,128)}) custom-call(f32[2,128,128]{2,1,0:T(8,128)S(1)} %get-tuple-element.4.new_obj, f32[2,16,2,2,4,128]{5,4,3,2,1,0:T(4,128)S(1)} %get-tuple-element.5.gathered), custom_call_target="tpu_custom_call" | custom-call | tf_op jit(solution)/shard_map/finish/pallas_call | solution.py:515
